TPU v7x, 256 devices: a whole 4x4x8 slice. The times are simulated.
256 devices in a mesh: gx: 64 (over z, x, core), gy: 4 (over y).
Axes of the slice: x: 4, y: 4, z: 8, core: 2. Of those that a mesh axis runs over, the one named last changes fastest.
Arguments:
- pressure: float32 [512, 512, 128], P('gx', 'gy'), may hold values from -6 to 8
- vel_y: float32 [512, 512, 128], P('gx', 'gy'), may hold values from -6 to 6
- vel_z: float32 [512, 512, 128], P('gx', 'gy'), may hold values from -6 to 6
- material: int32 [512, 512, 128], P('gx', 'gy'), may hold values from 0 to 7
- absorb_table: float32 [8], replicated, may hold values from 0.02 to 4
Outputs:
- pressure_next: float32 [512, 512, 128], P('gx', 'gy')
- vel_y_next: float32 [512, 512, 128], P('gx', 'gy')
- vel_z_next: float32 [512, 512, 128], P('gx', 'gy')
All inputs are finite; a program needn't handle non-finite values.
Results may differ from a plain program's by a relative error of at most 0.0004.
Values sent between devices are 32-bit elements; how exact they have to be, the bound alone decides.
A program may use at most 128 MiB of HBM per device.

v0:
```python
import jax
import jax.numpy as jnp
from jax import lax
from jax.sharding import PartitionSpec as P

MATS = 8


def passed_along(value, axis, steps):
    count = lax.axis_size(axis)
    first, last = (max(0, -steps), min(count, count - steps))
    return lax.ppermute(value, axis, [(source, source + steps) for source in range(first, last)])


def join_segments(left, right):
    denom = 1.0 - left[5] * right[1]
    inner_const = (left[3] + left[5] * right[0]) / denom
    inner_left = left[4] / denom
    inner_right = left[5] * right[2] / denom
    outer_const = right[0] + right[1] * inner_const
    outer_left = right[1] * inner_left
    outer_right = right[2] + right[1] * inner_right
    return (
        left[0] + left[2] * outer_const,
        left[1] + left[2] * outer_left,
        left[2] * outer_right,
        right[3] + right[4] * inner_const,
        right[4] * inner_left,
        right[5] + right[4] * inner_right,
    )


def sweep_lines(excess, stacked):

    def forward(carry, items):
        carried, value_prev = carry
        excess_row, value_row = items
        inverse = 1.0 / (1.0 + excess_row + carried)
        value = (value_row + value_prev) * inverse[None]
        carried_next = (excess_row + carried) * inverse
        return ((carried_next, value), (inverse, value))

    start = (jnp.ones(excess.shape[1:], jnp.float32), jnp.zeros(stacked.shape[1:], jnp.float32))
    _, (inverses, values) = lax.scan(forward, start, (excess, stacked))

    def backward(following, items):
        inverse, value = items
        current = value + inverse[None] * following
        return (current, current)

    _, solved = lax.scan(
        backward, jnp.zeros(stacked.shape[1:], jnp.float32), (inverses, values), reverse=True
    )
    return solved


def body(pressure, vel_y, vel_z, material, absorb_table):
    absorb = jnp.zeros(pressure.shape, jnp.float32)
    for entry in range(MATS):
        absorb = absorb + jnp.where(material == entry, absorb_table[entry], 0.0)
    damping = 1.0 / (1.0 + absorb)
    above = passed_along(pressure[:, :1, :], "gy", -1)
    upper_y = jnp.concatenate([pressure[:, 1:, :], above], axis=1)
    upper_z = jnp.concatenate([pressure[:, :, 1:], jnp.zeros_like(pressure[:, :, :1])], axis=2)
    vel_y_next = damping * (vel_y - 0.5 * (upper_y - pressure))
    vel_z_next = damping * (vel_z - 0.5 * (upper_z - pressure))
    below = passed_along(vel_y_next[:, -1:, :], "gy", 1)
    lower_y = jnp.concatenate([below, vel_y_next[:, :-1, :]], axis=1)
    lower_z = jnp.concatenate([jnp.zeros_like(pressure[:, :, :1]), vel_z_next[:, :, :-1]], axis=2)
    source = pressure - 0.5 * (vel_y_next - lower_y + vel_z_next - lower_z)
    line_cells = pressure.shape[0] * lax.axis_size("gx")
    coupling = 1.0 * (line_cells * line_cells // 4)
    excess = (1.0 + absorb) / coupling
    scaled = source / coupling
    rows = lax.broadcasted_iota(jnp.int32, pressure.shape, 0)
    first_unit = jnp.where(rows == 0, -1.0, 0.0)
    last_unit = jnp.where(rows == pressure.shape[0] - 1, -1.0, 0.0)
    stacked = jnp.stack([scaled, first_unit, last_unit], axis=1)
    solved = sweep_lines(excess, stacked)
    local_part = solved[:, 0]
    left_spike = solved[:, 1]
    right_spike = solved[:, 2]
    own = (
        local_part[0],
        -left_spike[0],
        -right_spike[0],
        local_part[-1],
        -left_spike[-1],
        -right_spike[-1],
    )
    nothing = jnp.zeros(local_part.shape[1:], jnp.float32)
    single = jnp.ones(local_part.shape[1:], jnp.float32)
    identity = (nothing, nothing, single, nothing, single, nothing)
    table = (
        lax.all_gather(own[0][None], "gx", axis=0, tiled=True),
        lax.all_gather(own[1][None], "gx", axis=0, tiled=True),
        lax.all_gather(own[2][None], "gx", axis=0, tiled=True),
        lax.all_gather(own[3][None], "gx", axis=0, tiled=True),
        lax.all_gather(own[4][None], "gx", axis=0, tiled=True),
        lax.all_gather(own[5][None], "gx", axis=0, tiled=True),
    )
    position = lax.axis_index("gx")
    indices = jnp.arange(lax.axis_size("gx"), dtype=jnp.int32)

    def take_lower(carry, items):
        index, pieces = items
        merged = join_segments(carry, pieces)
        keep = index < position
        return (tuple((jnp.where(keep, fresh, older) for fresh, older in zip(merged, carry))), None)

    def take_higher(carry, items):
        index, pieces = items
        merged = join_segments(pieces, carry)
        keep = index > position
        return (tuple((jnp.where(keep, fresh, older) for fresh, older in zip(merged, carry))), None)

    prefix, _ = lax.scan(take_lower, identity, (indices, table))
    suffix, _ = lax.scan(take_higher, identity, (indices, table), reverse=True)
    top_rhs = own[0] + own[1] * prefix[3] + own[2] * suffix[0]
    bottom_rhs = own[3] + own[4] * prefix[3] + own[5] * suffix[0]
    top_top = 1.0 - own[1] * prefix[5]
    top_bottom = -own[2] * suffix[1]
    bottom_top = -own[4] * prefix[5]
    bottom_bottom = 1.0 - own[5] * suffix[1]
    determinant = top_top * bottom_bottom - top_bottom * bottom_top
    top_value = (top_rhs * bottom_bottom - top_bottom * bottom_rhs) / determinant
    bottom_value = (top_top * bottom_rhs - bottom_top * top_rhs) / determinant
    before_value = prefix[3] + prefix[5] * top_value
    after_value = suffix[0] + suffix[1] * bottom_value
    pressure_next = local_part - left_spike * before_value[None] - right_spike * after_value[None]
    return (pressure_next, vel_y_next, vel_z_next)


def solution(mesh):
    return jax.shard_map(
        body,
        mesh=mesh,
        in_specs=(
            P("gx", "gy", None),
            P("gx", "gy", None),
            P("gx", "gy", None),
            P("gx", "gy", None),
            P(),
        ),
        out_specs=(P("gx", "gy", None), P("gx", "gy", None), P("gx", "gy", None)),
        check_vma=False,
    )
```

profile of v0, /device:TPU:1, one launch (start us, length us, event | category | flops | bytes accessed | tf_op | source)
XLA Modules:
  0.0 848.9 jit_solution(11246831425350953470)
XLA Ops:
  8.1 1.3 collective-permute-start
  9.4 1.6 fusion.49
  11.0 1.1 slice.93
  12.1 1.2 slice.97
  13.4 6.4 fusion.32
  19.8 4.6 collective-permute-start.1
  25.8 1.4 broadcast.68.clone
  27.2 20.3 %while.64 = (s32[]{:T(128)}, f32[128,128]{1,0:T(8,128)S(1)}, f32[3,128,128]{2,1,0:T(8,128)S(1)}, f32[8,128,128]{2,1,0:T(8,128)S(1)}, f32[8,3,128,128]{3,2,1,0:T(...) while((s32[]{:T(128)}, f32[128,128]{1,0:T(8,128)S(1)}, ...), condition=%wide.region_1.2_spmd.clone, body=%wide.region_0.1_spmd.clone.sunk | while | flops 262147 | bytes 1376881 | solution.py:44
  48.5 15.2 %while.65 = (s32[]{:T(128)}, f32[3,128,128]{2,1,0:T(8,128)S(1)}, f32[8,3,128,128]{3,2,1,0:T(8,128)S(1)}, f32[8,3,128,128]{3,2,1,0:T(8,128)}, f32[8,128,128]{2,1,0:T(8,128)}, /*index=5*/s32[]{:T(128)}, s32[]{:T(128)}, s32[]{:T(128)}) while((s32[]{:T(128)}, f32[3,128,128]{2,1,0:T(8,128)S(1)}, f32[8,3,128,128]{3,2,1,0:T(8,128)S(1)}, ...), condition=%wide.region_3.4_spmd.clone, body=%wide.region_2.3_spmd.clone.sunk | while | flops 147460 | bytes 983155 | solution.py:51
  67.7 81.3 %all-gather.13.cloned.1.call-done = f32[64,1,128,128]{3,2,1,0:T(8,128)} async-done(((f32[1,1,128,128]{3,2,1,0:T(8,128)}), f32[64,1,128,128]{3,2,1,0:T(8,128)}) %all-gather.13.cloned.1.call-update) | async-done | bytes 4194320 | tf_op jit(solution)/shard_map/all_gather | solution.py:98
  149.1 79.5 %all-gather.15.cloned.1.call-done = f32[64,1,128,128]{3,2,1,0:T(8,128)} async-done(((f32[1,1,128,128]{3,2,1,0:T(8,128)}), f32[64,1,128,128]{3,2,1,0:T(8,128)}) %all-gather.15.cloned.1.call-update) | async-done | bytes 4194320 | tf_op jit(solution)/shard_map/all_gather | solution.py:99
  228.6 79.0 %all-gather.17.cloned.1.call-done = f32[64,1,128,128]{3,2,1,0:T(8,128)} async-done(((f32[1,1,128,128]{3,2,1,0:T(8,128)}), f32[64,1,128,128]{3,2,1,0:T(8,128)}) %all-gather.17.cloned.1.call-update) | async-done | bytes 4194320 | tf_op jit(solution)/shard_map/all_gather | solution.py:95
  307.6 78.8 %all-gather.19.cloned.1.call-done = f32[64,1,128,128]{3,2,1,0:T(8,128)} async-done(((f32[1,1,128,128]{3,2,1,0:T(8,128)}), f32[64,1,128,128]{3,2,1,0:T(8,128)}) %all-gather.19.cloned.1.call-update) | async-done | bytes 4194320 | tf_op jit(solution)/shard_map/all_gather | solution.py:96
  386.4 78.8 %all-gather.21.cloned.1.call-done = f32[64,1,128,128]{3,2,1,0:T(8,128)} async-done(((f32[1,1,128,128]{3,2,1,0:T(8,128)}), f32[64,1,128,128]{3,2,1,0:T(8,128)}) %all-gather.21.cloned.1.call-update) | async-done | bytes 4194320 | tf_op jit(solution)/shard_map/all_gather | solution.py:100
  465.2 78.8 %all-gather.23.cloned.1.call-done = f32[64,1,128,128]{3,2,1,0:T(8,128)} async-done(((f32[1,1,128,128]{3,2,1,0:T(8,128)}), f32[64,1,128,128]{3,2,1,0:T(8,128)}) %all-gather.23.cloned.1.call-update) | async-done | bytes 4194320 | tf_op jit(solution)/shard_map/all_gather | solution.py:97
  544.0 148.7 %while.67 = (s32[]{:T(128)}, f32[128,128]{1,0:T(8,128)S(1)}, f32[128,128]{1,0:T(8,128)S(1)}, s32[64]{0:T(128)S(1)}, s32[]{:T(128)}, /*index=5*/f32[64,128,128]{2...) while((s32[]{:T(128)}, f32[128,128]{1,0:T(8,128)S(1)}, ...), condition=%wide.region_7.8_spmd.clone, body=%wide.region_6.7_spmd.clone.sunk | while | flops 278533 | bytes 655541 | solution.py:118
  545.3 1.1 fusion.56
  547.6 1.1 fusion.56
  549.9 1.1 fusion.56
  552.3 1.1 fusion.56
  554.6 1.1 fusion.56
  556.9 1.1 fusion.56
  559.2 1.1 fusion.56
  692.7 148.3 %while.66 = (s32[]{:T(128)}, f32[128,128]{1,0:T(8,128)S(1)}, f32[128,128]{1,0:T(8,128)S(1)}, s32[64]{0:T(128)S(1)}, s32[]{:T(128)}, /*index=5*/f32[64,128,128]{2...) while((s32[]{:T(128)}, f32[128,128]{1,0:T(8,128)S(1)}, ...), condition=%wide.region_5.6_spmd.clone, body=%wide.region_4.5_spmd.clone.sunk | while | flops 245764 | bytes 655521 | solution.py:117
  (339 shorter events, 246.4 us)
Async XLA Ops:
  7.2 6.2 copy-start
  7.2 6.2 copy-start.4
  7.2 6.2 copy-start.5
  7.2 141.9 %all-gather.13.cloned.1.call-start = ((), (), s32[]{:S(2)}) async-start(), calls=%async_computation | async-start | bytes 4259840 | tf_op jit(solution)/shard_map/all_gather | solution.py:98
  7.2 6.2 copy-start.6
  8.1 5.2 collective-permute-start
  19.8 5.7 copy-start.1
  19.8 5.7 copy-start.2
  19.8 5.4 collective-permute-start.1
  47.5 0.8 copy-start.3
  64.5 164.2 %all-gather.15.cloned.1.call-start = ((), (), s32[]{:S(2)}) async-start(), calls=%async_computation.1 | async-start | bytes 4259840 | tf_op jit(solution)/shard_map/all_gather | solution.py:99
  65.2 242.4 %all-gather.17.cloned.1.call-start = ((), (), s32[]{:S(2)}) async-start(), calls=%async_computation.2 | async-start | bytes 4259840 | tf_op jit(solution)/shard_map/all_gather | solution.py:95
  65.9 320.5 %all-gather.19.cloned.1.call-start = ((), (), s32[]{:S(2)}) async-start(), calls=%async_computation.3 | async-start | bytes 4259840 | tf_op jit(solution)/shard_map/all_gather | solution.py:96
  66.5 398.7 %all-gather.21.cloned.1.call-start = ((), (), s32[]{:S(2)}) async-start(), calls=%async_computation.4 | async-start | bytes 4259840 | tf_op jit(solution)/shard_map/all_gather | solution.py:100
  67.1 476.9 %all-gather.23.cloned.1.call-start = ((), (), s32[]{:S(2)}) async-start(), calls=%async_computation.5 | async-start | bytes 4259840 | tf_op jit(solution)/shard_map/all_gather | solution.py:97
Sparse Core Ops, SparseCore 0:
  64.6 84.4 all-gather.12
  152.4 76.1 all-gather.14
  231.4 76.1 all-gather.16
  310.2 76.1 all-gather.18
  389.0 76.1 all-gather.20
  467.8 76.1 all-gather.22
where the time goes:
time: 859 us; the launch traced here: 849 us
  waiting for transfers between devices  480 us (56%)
  other arithmetic  172 us (20%)
  local copies, waits for them, and re-layouts  89.3 us (10%)
  loops' own time  86.8 us (10%)
  between operations  14.4 us (2%)
    all_gather x1, waiting for transfers between devices, body(): lax.all_gather(own[3][None], 'gx', axis=0, tiled=True)  81.3 us
    all_gather x1, waiting for transfers between devices, body(): lax.all_gather(own[4][None], 'gx', axis=0, tiled=True)  79.5 us
    all_gather x1, waiting for transfers between devices, body(): lax.all_gather(own[0][None], 'gx', axis=0, tiled=True)  79 us
    all_gather x1, waiting for transfers between devices, body(): lax.all_gather(own[2][None], 'gx', axis=0, tiled=True)  78.8 us
    all_gather x1, waiting for transfers between devices, body(): lax.all_gather(own[1][None], 'gx', axis=0, tiled=True)  78.8 us
    all_gather x1, waiting for transfers between devices, body(): lax.all_gather(own[5][None], 'gx', axis=0, tiled=True)  78.8 us
    dynamic_slice x128, local copies, waits for them, and re-layouts, body(): prefix, _ = lax.scan(take_lower, identity, (indices, table))  75.1 us
    select_n x64, other arithmetic, take_higher(): jnp.where(keep, fresh, older)  67.8 us
  transfers between devices with their start and end apart: 8, of which 7 were waited for; matrix products, arithmetic and copies ran while one was open for 0% of the time, Pallas kernels for 0%

commit v1 on v0

--- a/solution.py
+++ b/solution.py
@@ -4,6 +4,11 @@
 from jax.sharding import PartitionSpec as P
 
 MATS = 8
+
+
+def swapped_in(array, axis, along):
+    repeated = jnp.stack([array] * lax.axis_size(axis))
+    return jnp.concatenate(lax.all_to_all(repeated, axis, 0, 0), axis=along)
 
 
 def passed_along(value, axis, steps):
@@ -94,7 +99,7 @@
     table = (
         lax.all_gather(own[0][None], "gx", axis=0, tiled=True),
         lax.all_gather(own[1][None], "gx", axis=0, tiled=True),
-        lax.all_gather(own[2][None], "gx", axis=0, tiled=True),
+        swapped_in(own[2][None], "gx", 0),
         lax.all_gather(own[3][None], "gx", axis=0, tiled=True),
         lax.all_gather(own[4][None], "gx", axis=0, tiled=True),
         lax.all_gather(own[5][None], "gx", axis=0, tiled=True),

time: 859 us -> 801 us (0.932)
  waiting for transfers between devices: 480 us -> 406 us
  starting transfers between devices: 6.16 us -> 19.8 us
    all_to_all x0 -> x1, waiting for transfers between devices: none -> 106 us  [swapped_in(): return jnp.concatenate(lax.all_to_all(repeated, axis, 0, 0), axis=along)]
    all_gather x1, waiting for transfers between devices: 81.3 us -> 0.01 us  [body(): lax.all_gather(own[3][None], 'gx', axis=0, tiled=True)]
    all_gather x1 -> x0, waiting for transfers between devices: 78.8 us -> none  [body(): lax.all_gather(own[2][None], 'gx', axis=0, tiled=True)]
    all_gather x1, waiting for transfers between devices: 79.5 us -> 60.5 us  [body(): lax.all_gather(own[4][None], 'gx', axis=0, tiled=True)]
    all_to_all x0 -> x1, starting transfers between devices: none -> 13.6 us  [swapped_in(): return jnp.concatenate(lax.all_to_all(repeated, axis, 0, 0), axis=along)]
  transfers between devices with their start and end apart: 8 -> 8, of which waited for: 7 -> 6; matrix products, arithmetic and copies ran while one was open for 0% -> 1% of each run, Pallas kernels for 0% -> 0%
where the time goes in v1:
time: 801 us; the launch traced here: 791 us
  waiting for transfers between devices  406 us (51%)
  other arithmetic  172 us (21%)
  local copies, waits for them, and re-layouts  91.8 us (11%)
  loops' own time  86.8 us (11%)
  starting transfers between devices  19.8 us (2%)
  between operations  14.1 us (2%)
    all_to_all x1, waiting for transfers between devices, swapped_in(): return jnp.concatenate(lax.all_to_all(repeated, axis, 0, 0), axis=along)  106 us
    all_gather x1, waiting for transfers between devices, body(): lax.all_gather(own[0][None], 'gx', axis=0, tiled=True)  79 us
    all_gather x1, waiting for transfers between devices, body(): lax.all_gather(own[1][None], 'gx', axis=0, tiled=True)  78.8 us
    all_gather x1, waiting for transfers between devices, body(): lax.all_gather(own[5][None], 'gx', axis=0, tiled=True)  78.8 us
    dynamic_slice x128, local copies, waits for them, and re-layouts, body(): prefix, _ = lax.scan(take_lower, identity, (indices, table))  75.1 us
    select_n x64, other arithmetic, take_higher(): jnp.where(keep, fresh, older)  67.8 us
    select_n x64, other arithmetic, take_lower(): jnp.where(keep, fresh, older)  67.8 us
    all_gather x1, waiting for transfers between devices, body(): lax.all_gather(own[4][None], 'gx', axis=0, tiled=True)  60.5 us
  transfers between devices with their start and end apart: 8, of which 6 were waited for; matrix products, arithmetic and copies ran while one was open for 1% of the time, Pallas kernels for 0%

profile of v1, /device:TPU:1, one launch (start us, length us, event | category | flops | bytes accessed | tf_op | source)
XLA Modules:
  0.0 791.0 jit_solution(223411861730702953)
XLA Ops:
  8.1 1.3 collective-permute-start
  9.4 1.6 fusion.49
  11.0 1.1 slice.93
  12.1 1.2 slice.97
  13.4 6.3 fusion.32
  19.8 4.6 collective-permute-start.1
  25.8 1.4 broadcast.70.clone
  27.2 20.3 %while.64 = (s32[]{:T(128)}, f32[128,128]{1,0:T(8,128)S(1)}, f32[3,128,128]{2,1,0:T(8,128)S(1)}, f32[8,128,128]{2,1,0:T(8,128)S(1)}, f32[8,3,128,128]{3,2,1,0:T(...) while((s32[]{:T(128)}, f32[128,128]{1,0:T(8,128)S(1)}, ...), condition=%wide.region_1.2_spmd.clone, body=%wide.region_0.1_spmd.clone.sunk | while | flops 262147 | bytes 1376881 | solution.py:49
  48.5 15.2 %while.65 = (s32[]{:T(128)}, f32[3,128,128]{2,1,0:T(8,128)S(1)}, f32[8,3,128,128]{3,2,1,0:T(8,128)S(1)}, f32[8,3,128,128]{3,2,1,0:T(8,128)}, f32[8,128,128]{2,1,0:T(8,128)}, /*index=5*/s32[]{:T(128)}, s32[]{:T(128)}, s32[]{:T(128)}) while((s32[]{:T(128)}, f32[3,128,128]{2,1,0:T(8,128)S(1)}, f32[8,3,128,128]{3,2,1,0:T(8,128)S(1)}, ...), condition=%wide.region_3.4_spmd.clone, body=%wide.region_2.3_spmd.clone.sunk | while | flops 147460 | bytes 983155 | solution.py:56
  66.5 2.5 stack.16
  69.0 13.6 %all-to-all-start = ((f32[64,1,128,128]{3,2,1,0:T(8,128)}), f32[64,1,128,128]{3,2,1,0:T(8,128)}, u32[]{:S(2)}, u32[]{:S(2)}) async-start(f32[64,1,128,128]{3,2,1,0:T(8,128)} %stack.16), calls=%async_computation | async-start | bytes 8388608 | tf_op jit(solution)/shard_map/all_to_all | solution.py:11
  83.3 105.9 %all-to-all-done = f32[64,1,128,128]{3,2,1,0:T(8,128)} async-done(((f32[64,1,128,128]{3,2,1,0:T(8,128)}), f32[64,1,128,128]{3,2,1,0:T(8,128)}, u32[]{:S(2)}, u32[]{:S(2)}) %all-to-all-start) | async-done | bytes 4194336 | tf_op jit(solution)/shard_map/all_to_all | solution.py:11
  189.2 60.5 %all-gather.13.cloned.1.call-done = f32[64,1,128,128]{3,2,1,0:T(8,128)} async-done(((f32[1,1,128,128]{3,2,1,0:T(8,128)}), f32[64,1,128,128]{3,2,1,0:T(8,128)}) %all-gather.13.cloned.1.call-update) | async-done | bytes 4194320 | tf_op jit(solution)/shard_map/all_gather | solution.py:104
  249.7 79.0 %all-gather.15.cloned.1.call-done = f32[64,1,128,128]{3,2,1,0:T(8,128)} async-done(((f32[1,1,128,128]{3,2,1,0:T(8,128)}), f32[64,1,128,128]{3,2,1,0:T(8,128)}) %all-gather.15.cloned.1.call-update) | async-done | bytes 4194320 | tf_op jit(solution)/shard_map/all_gather | solution.py:100
  328.6 78.8 %all-gather.17.cloned.1.call-done = f32[64,1,128,128]{3,2,1,0:T(8,128)} async-done(((f32[1,1,128,128]{3,2,1,0:T(8,128)}), f32[64,1,128,128]{3,2,1,0:T(8,128)}) %all-gather.17.cloned.1.call-update) | async-done | bytes 4194320 | tf_op jit(solution)/shard_map/all_gather | solution.py:101
  407.5 78.8 %all-gather.19.cloned.1.call-done = f32[64,1,128,128]{3,2,1,0:T(8,128)} async-done(((f32[1,1,128,128]{3,2,1,0:T(8,128)}), f32[64,1,128,128]{3,2,1,0:T(8,128)}) %all-gather.19.cloned.1.call-update) | async-done | bytes 4194320 | tf_op jit(solution)/shard_map/all_gather | solution.py:105
  486.3 148.7 %while.67 = (s32[]{:T(128)}, f32[128,128]{1,0:T(8,128)S(1)}, f32[128,128]{1,0:T(8,128)S(1)}, s32[64]{0:T(128)S(1)}, s32[]{:T(128)}, /*index=5*/f32[64,128,128]{2...) while((s32[]{:T(128)}, f32[128,128]{1,0:T(8,128)S(1)}, ...), condition=%wide.region_7.8_spmd.clone, body=%wide.region_6.7_spmd.clone.sunk | while | flops 278533 | bytes 655541 | solution.py:123
  487.5 1.1 fusion.56
  489.8 1.1 fusion.56
  492.2 1.1 fusion.56
  494.5 1.1 fusion.56
  496.8 1.1 fusion.56
  499.1 1.1 fusion.56
  635.0 148.5 %while.66 = (s32[]{:T(128)}, f32[128,128]{1,0:T(8,128)S(1)}, f32[128,128]{1,0:T(8,128)S(1)}, s32[64]{0:T(128)S(1)}, s32[]{:T(128)}, /*index=5*/f32[64,128,128]{2...) while((s32[]{:T(128)}, f32[128,128]{1,0:T(8,128)S(1)}, ...), condition=%wide.region_5.6_spmd.clone, body=%wide.region_4.5_spmd.clone.sunk | while | flops 245764 | bytes 655521 | solution.py:122
  (339 shorter events, 247.1 us)
Async XLA Ops:
  7.2 6.2 copy-start
  7.2 6.2 copy-start.4
  7.2 6.2 copy-start.5
  7.2 182.0 %all-gather.11.cloned.1.call-start = ((), (), s32[]{:S(2)}) async-start(), calls=%async_computation.1 | async-start | bytes 4259840 | tf_op jit(solution)/shard_map/all_gather | solution.py:103
  7.2 6.2 copy-start.6
  8.1 5.2 collective-permute-start
  19.8 5.7 copy-start.1
  19.8 5.7 copy-start.2
  19.8 5.4 collective-permute-start.1
  47.5 0.8 copy-start.3
  64.5 185.2 %all-gather.13.cloned.1.call-start = ((), (), s32[]{:S(2)}) async-start(), calls=%async_computation.2 | async-start | bytes 4259840 | tf_op jit(solution)/shard_map/all_gather | solution.py:104
  65.2 263.4 %all-gather.15.cloned.1.call-start = ((), (), s32[]{:S(2)}) async-start(), calls=%async_computation.3 | async-start | bytes 4259840 | tf_op jit(solution)/shard_map/all_gather | solution.py:100
  65.9 341.5 %all-gather.17.cloned.1.call-start = ((), (), s32[]{:S(2)}) async-start(), calls=%async_computation.4 | async-start | bytes 4259840 | tf_op jit(solution)/shard_map/all_gather | solution.py:101
  69.0 120.2 %all-to-all-start = ((f32[64,1,128,128]{3,2,1,0:T(8,128)}), f32[64,1,128,128]{3,2,1,0:T(8,128)}, u32[]{:S(2)}, u32[]{:S(2)}) async-start(f32[64,1,128,128]{3,2,1,0:T(8,128)} %stack.16), calls=%async_computation | async-start | bytes 8388608 | tf_op jit(solution)/shard_map/all_to_all | solution.py:11
  82.7 403.6 %all-gather.19.cloned.1.call-start = ((), (), s32[]{:S(2)}) async-start(), calls=%async_computation.5 | async-start | bytes 4259840 | tf_op jit(solution)/shard_map/all_gather | solution.py:105
Sparse Core Ops, SparseCore 0:
  64.6 102.8 all-gather.10
  170.8 78.8 all-gather.12
  252.4 76.1 all-gather.14
  331.3 76.1 all-gather.16
  410.1 76.1 all-gather.18
